TPU v7x, 32 devices: a whole 2x2x4 slice. The times are simulated.
32 devices in a mesh: dp: 4 (over z), ctx: 8 (over y, x, core).
Axes of the slice: x: 2, y: 2, z: 4, core: 2. Of those that a mesh axis runs over, the one named last changes fastest.
Arguments:
- inputs: bfloat16 [4, 1024, 1024], P('dp', 'ctx'), may hold values from -6 to 6
- cotangent: bfloat16 [4, 1024, 1024], P('dp', 'ctx'), may hold values from -6 to 6
- mixer_params: float32 [4194304], P(('dp', 'ctx')), may hold values from -0.1875 to 0.1875
- mixer_first: float32 [4194304], P(('dp', 'ctx')), may hold values from -0.0014648438 to 0.0014648438
- mixer_second: float32 [4194304], P(('dp', 'ctx')), may hold values from 2.3434208e-11 to 2.3434207e-10
- ffn_params: float32 [4325376], P(('dp', 'ctx')), may hold values from -0.21320072 to 0.21320072
- ffn_first: float32 [4325376], P(('dp', 'ctx')), may hold values from -0.0014648438 to 0.0014648438
- ffn_second: float32 [4325376], P(('dp', 'ctx')), may hold values from 2.3434208e-11 to 2.3434207e-10
- small_params: float32 [14852], replicated, may hold values from -7 to 2.8
- small_first: float32 [14852], replicated, may hold values from -0.0014648438 to 0.0014648438
- small_second: float32 [14852], replicated, may hold values from 2.3434208e-11 to 2.3434208e-07
Outputs:
- outputs: bfloat16 [4, 1024, 1024], P('dp', 'ctx')
- grad_inputs: bfloat16 [4, 1024, 1024], P('dp', 'ctx')
- mixer_grad: float32 [4194304], P(('dp', 'ctx'))
- ffn_grad: float32 [4325376], P(('dp', 'ctx'))
- small_grad: float32 [14852], replicated
- mixer_new: float32 [4194304], P(('dp', 'ctx'))
- mixer_first_new: float32 [4194304], P(('dp', 'ctx'))
- mixer_second_new: float32 [4194304], P(('dp', 'ctx'))
- ffn_new: float32 [4325376], P(('dp', 'ctx'))
- ffn_first_new: float32 [4325376], P(('dp', 'ctx'))
- ffn_second_new: float32 [4325376], P(('dp', 'ctx'))
- small_new: float32 [14852], replicated
- small_first_new: float32 [14852], replicated
- small_second_new: float32 [14852], replicated
All inputs are finite; a program needn't handle non-finite values.
Results may differ from a plain program's by a relative error of at most 0.013.
Values may be sent and summed in bfloat16 or wider, within the bound.
A program may use at most 320 MiB of HBM per device.

v0:
```python
import jax
import jax.numpy as jnp
from jax import lax
from jax.sharding import PartitionSpec as P

D = 1024
H = 2
DK = 256
DV = 512
FF = 1408
CONV = 4
GROUP = 64
EPSILON = 1e-06
ADAM_EPS = 1e-08
LEARN_RATE = 0.02
BETA_ONE = 0.9
BETA_TWO = 0.999
DECAY_RATE = 0.1
CORRECT_ONE = 1.0 - 0.9**3
CORRECT_TWO = 1.0 - 0.999**3
MAX_NORM = 1.0
HIGHEST = lax.Precision.HIGHEST


def from_behind(value, axis, steps):
    count = lax.axis_size(axis)
    initial, last = (max(0, -steps), min(count, count - steps))
    return lax.ppermute(value, axis, [(source, source + steps) for source in range(initial, last)])


def entering(array, axis, combine, identity):
    devices, position = (lax.axis_size(axis), lax.axis_index(axis))
    everything = jax.tree.map(
        lambda part, kind: lax.all_gather(part.astype(kind), axis),
        array,
        (jnp.bfloat16, jnp.bfloat16),
    )
    start = jax.tree.map(
        lambda part, zero: jnp.broadcast_to(jnp.asarray(zero, part.dtype), part.shape),
        array,
        identity,
    )

    def lap(k, before):
        reached = k < position
        new = combine(
            before, jax.tree.map(lambda part, own: part[k].astype(own.dtype), everything, array)
        )
        return jax.tree.map(lambda a, b: jnp.where(reached, a, b), new, before)

    return lax.fori_loop(0, devices, lap, start)


def carried_in(array, axis, join, neutral):
    count = lax.axis_size(axis)
    place = lax.axis_index(axis)
    ahead = count - 1 - place
    gathered = jax.tree.map(
        lambda a, kind: lax.all_gather(a.astype(kind), axis),
        array,
        jax.tree.map(lambda a: jnp.bfloat16 if a.dtype == jnp.float32 else a.dtype, array),
    )
    state = jax.tree.map(lambda a, e: jnp.zeros_like(a) + jnp.asarray(e, a.dtype), array, neutral)

    def one(lap, state):
        source = count - 1 - lap
        return join(
            state,
            jax.tree.map(
                lambda a, own: lax.dynamic_index_in_dim(a, source, 0, False).astype(own.dtype),
                gathered,
                array,
            ),
        )

    return lax.fori_loop(0, ahead, one, state)


def norm_scale(values, gain):
    return values * lax.rsqrt(jnp.mean(values * values, axis=-1, keepdims=True) + EPSILON) * gain


def swiglu(gate_part, up_part):
    return jax.nn.silu(gate_part) * up_part


def unpack_small(packed):
    width = 2 * H * DK + H * DV
    lengths = [D, D, DV, CONV * width, D * 2 * H, H, H]
    pieces = []
    offset = 0
    for length in lengths:
        pieces.append(packed[offset : offset + length])
        offset = offset + length
    return (
        pieces[0],
        pieces[1],
        pieces[2],
        pieces[3].reshape(CONV, width),
        pieces[4].reshape(D, 2 * H),
        pieces[5],
        pieces[6],
    )


def split_weights(mix_whole, ffn_whole):
    mix_rows = mix_whole.reshape(-1, D)
    ffn_rows = ffn_whole.reshape(-1, D)
    edge = 2 * H * DK + 2 * H * DV
    return (mix_rows[:edge], mix_rows[edge:], ffn_rows[: 2 * FF], ffn_rows[2 * FF :])


def features(extended, tap_values, gate_logits, a_log, dt_bias):
    count = extended.shape[0] - (CONV - 1)
    summed = tap_values[0] * extended[0:count]
    for tap_index in range(1, CONV):
        summed = summed + tap_values[tap_index] * extended[tap_index : tap_index + count]
    activated = jax.nn.silu(summed)
    query_part = activated[:, : H * DK].reshape(count, H, DK)
    key_part = activated[:, H * DK : 2 * H * DK].reshape(count, H, DK)
    value_part = activated[:, 2 * H * DK :].reshape(count, H, DV)
    query = (
        query_part
        * lax.rsqrt(jnp.sum(query_part * query_part, axis=-1, keepdims=True) + EPSILON)
        * DK ** (-0.5)
    )
    keys = key_part * lax.rsqrt(jnp.sum(key_part * key_part, axis=-1, keepdims=True) + EPSILON)
    beta = jax.nn.sigmoid(gate_logits[:, :H])
    decay = -jnp.exp(a_log) * jax.nn.softplus(gate_logits[:, H:] + dt_bias)
    return (
        jnp.transpose(query, (1, 0, 2)),
        jnp.transpose(keys, (1, 0, 2)),
        jnp.transpose(value_part, (1, 0, 2)),
        beta.T,
        decay.T,
    )


def split_groups(values):
    blocks = values.shape[1] // GROUP
    shaped = values.reshape((values.shape[0], blocks, GROUP) + values.shape[2:])
    return jnp.moveaxis(shaped, 1, 0)


def group_parts(key_block, value_block, beta_block, decay_block):
    size = decay_block.shape[-1]
    cumulative = jnp.cumsum(decay_block, axis=-1)
    row_index = lax.broadcasted_iota(jnp.int32, (size, size), 0)
    col_index = lax.broadcasted_iota(jnp.int32, (size, size), 1)
    lower = row_index >= col_index
    strict = row_index > col_index
    spread = jnp.where(lower, cumulative[:, :, None] - cumulative[:, None, :], 0.0)
    decay_matrix = jnp.where(lower, jnp.exp(spread), 0.0)
    key_gram = jnp.einsum("hid,hjd->hij", key_block, key_block, precision=HIGHEST)
    system = jnp.where(strict, beta_block[:, :, None] * key_gram * decay_matrix, 0.0) + jnp.eye(
        size, dtype=key_block.dtype
    )
    right_side = jnp.concatenate(
        [
            key_block * (beta_block * jnp.exp(cumulative))[:, :, None],
            value_block * beta_block[:, :, None],
        ],
        axis=-1,
    )
    solved = jax.scipy.linalg.solve_triangular(system, right_side, lower=True, unit_diagonal=True)
    key_mix = solved[..., :DK]
    value_mix = solved[..., DK:]
    last_decay = cumulative[:, -1]
    keys_to_end = key_block * jnp.exp(last_decay[:, None] - cumulative)[:, :, None]
    return (cumulative, decay_matrix, key_mix, value_mix, last_decay, keys_to_end)


def group_run(state, pieces):
    query_block, key_block, value_block, beta_block, decay_block = pieces
    cumulative, decay_matrix, key_mix, value_mix, last_decay, keys_to_end = group_parts(
        key_block, value_block, beta_block, decay_block
    )
    pseudo_values = value_mix - jnp.einsum("hcd,hde->hce", key_mix, state, precision=HIGHEST)
    scores = jnp.einsum("hid,hjd->hij", query_block, key_block, precision=HIGHEST) * decay_matrix
    block_out = jnp.einsum(
        "hcd,hde->hce", query_block * jnp.exp(cumulative)[:, :, None], state, precision=HIGHEST
    )
    block_out = block_out + jnp.einsum("hij,hje->hie", scores, pseudo_values, precision=HIGHEST)
    next_state = jnp.exp(last_decay)[:, None, None] * state + jnp.einsum(
        "hcd,hce->hde", keys_to_end, pseudo_values, precision=HIGHEST
    )
    return (next_state, block_out)


def mixer_run(state, query, keys, values, beta, decay):
    pieces = (
        split_groups(query),
        split_groups(keys),
        split_groups(values),
        split_groups(beta),
        split_groups(decay),
    )
    final_state, blocks_out = lax.scan(group_run, state, pieces)
    joined = jnp.moveaxis(blocks_out, 0, 1)
    return (joined.reshape(joined.shape[0], -1, joined.shape[-1]), final_state)


def combine(earlier, later):
    first_map, first_shift = earlier
    second_map, second_shift = later
    composed = jnp.einsum("hij,hjk->hik", second_map, first_map, precision=HIGHEST)
    shifted = jnp.einsum("hij,hjk->hik", second_map, first_shift, precision=HIGHEST) + second_shift
    return (composed, shifted)


def transition(keys, values, beta, decay):
    pieces = (split_groups(keys), split_groups(values), split_groups(beta), split_groups(decay))
    start = (
        jnp.broadcast_to(jnp.eye(DK, dtype=jnp.float32), (H, DK, DK)),
        jnp.zeros((H, DK, DV), jnp.float32),
    )

    def step_block(carry, piece):
        key_block, value_block, beta_block, decay_block = piece
        cumulative, decay_matrix, key_mix, value_mix, last_decay, keys_to_end = group_parts(
            key_block, value_block, beta_block, decay_block
        )
        block_map = jnp.exp(last_decay)[:, None, None] * jnp.eye(
            DK, dtype=key_block.dtype
        ) - jnp.einsum("hcd,hce->hde", keys_to_end, key_mix, precision=HIGHEST)
        block_shift = jnp.einsum("hcd,hce->hde", keys_to_end, value_mix, precision=HIGHEST)
        return (combine(carry, (block_map, block_shift)), None)

    result, unused = lax.scan(step_block, start, pieces)
    return result


def gated_norm(mixed, out_gate, gain_head):
    count = out_gate.shape[0]
    heads = jnp.transpose(mixed, (1, 0, 2))
    normed = norm_scale(heads, gain_head)
    return (normed * jax.nn.silu(out_gate.reshape(count, H, DV))).reshape(count, H * DV)


def adam_step(weight, grad_full, first, second, clip):
    grad_clipped = grad_full * clip
    first_new = BETA_ONE * first + (1.0 - BETA_ONE) * grad_clipped
    second_new = BETA_TWO * second + (1.0 - BETA_TWO) * grad_clipped * grad_clipped
    update = (
        first_new / CORRECT_ONE / (jnp.sqrt(second_new / CORRECT_TWO) + ADAM_EPS)
        + DECAY_RATE * weight
    )
    return (weight - LEARN_RATE * update, first_new, second_new)


def body(
    inputs,
    cotangent,
    mixer_params,
    mixer_first,
    mixer_second,
    ffn_params,
    ffn_first,
    ffn_second,
    small_params,
    small_first,
    small_second,
):
    gain_one, gain_two, gain_head, tap_values, w_gates, a_log, dt_bias = unpack_small(small_params)
    width = tap_values.shape[1]
    mix_part = mixer_params.astype(jnp.bfloat16)
    ffn_part = ffn_params.astype(jnp.bfloat16)
    mix_whole, ffn_whole = (
        lax.all_gather(mix_part, ("dp", "ctx"), axis=0, tiled=True),
        lax.all_gather(ffn_part, ("dp", "ctx"), axis=0, tiled=True),
    )
    w_in, w_out, w_ffn, w_down = split_weights(mix_whole, ffn_whole)
    x_float = inputs[0].astype(jnp.float32)
    count = x_float.shape[0]
    normed_in = norm_scale(x_float, gain_one).astype(jnp.bfloat16)
    projected = jnp.dot(normed_in, w_in.T, preferred_element_type=jnp.float32)
    gate_logits = jnp.dot(normed_in.astype(jnp.float32), w_gates, precision=HIGHEST)
    conv_pre = projected[:, :width]
    out_gate = projected[:, width:]
    border = from_behind(conv_pre[count - (CONV - 1) :], "ctx", 1)
    extended = jnp.concatenate([border, conv_pre], axis=0)
    query, keys, values, beta, decay = features(extended, tap_values, gate_logits, a_log, dt_bias)
    maps = transition(keys, values, beta, decay)
    eye_stack = jnp.broadcast_to(jnp.eye(DK, dtype=jnp.float32), (H, DK, DK))
    zero_stack = jnp.zeros((H, DK, DV), jnp.float32)
    prefix = entering((maps[0], maps[1]), "ctx", combine, (eye_stack, zero_stack))
    state_in = prefix[1]
    mixed, final_state = mixer_run(state_in, query, keys, values, beta, decay)
    head_out = gated_norm(mixed, out_gate, gain_head).astype(jnp.bfloat16)
    resid = x_float + jnp.dot(head_out, w_out, preferred_element_type=jnp.float32)
    normed_mid = norm_scale(resid, gain_two).astype(jnp.bfloat16)
    ffn_pre = jnp.dot(normed_mid, w_ffn.T, preferred_element_type=jnp.float32)
    gate_part = ffn_pre[:, :FF]
    up_part = ffn_pre[:, FF:]
    hidden_act = swiglu(gate_part, up_part).astype(jnp.bfloat16)
    result = (resid + jnp.dot(hidden_act, w_down, preferred_element_type=jnp.float32)).astype(
        jnp.bfloat16
    )
    seq_grad = cotangent[0]
    grad_float = seq_grad.astype(jnp.float32)
    grad_down = jnp.dot(hidden_act.T, seq_grad, preferred_element_type=jnp.float32)
    grad_hidden = jnp.dot(seq_grad, w_down.T, preferred_element_type=jnp.float32)
    unused_one, pull_swiglu = jax.vjp(swiglu, gate_part, up_part)
    grad_gate, grad_up = pull_swiglu(grad_hidden)
    grad_pre = jnp.concatenate([grad_gate, grad_up], axis=1).astype(jnp.bfloat16)
    grad_ffn = jnp.dot(grad_pre.T, normed_mid, preferred_element_type=jnp.float32)
    grad_mid = jnp.dot(grad_pre, w_ffn, preferred_element_type=jnp.float32)
    unused_two, pull_mid = jax.vjp(norm_scale, resid, gain_two)
    grad_through, grad_gain_two = pull_mid(grad_mid)
    grad_resid = grad_float + grad_through
    ffn_flat = jnp.concatenate([grad_ffn, grad_down], axis=0).reshape(-1)
    ffn_shard = lax.psum_scatter(ffn_flat, ("dp", "ctx"), scatter_dimension=0, tiled=True)
    resid_half = grad_resid.astype(jnp.bfloat16)
    grad_out = jnp.dot(head_out.T, resid_half, preferred_element_type=jnp.float32)
    grad_head = jnp.dot(resid_half, w_out.T, preferred_element_type=jnp.float32)
    unused_three, pull_gated = jax.vjp(gated_norm, mixed, out_gate, gain_head)
    grad_mixed, grad_gate_out, grad_gain_head = pull_gated(grad_head)
    unused_four, pull_mixer = jax.vjp(mixer_run, state_in, query, keys, values, beta, decay)
    local_term = pull_mixer((grad_mixed, jnp.zeros_like(final_state)))[0]
    flipped = jnp.transpose(maps[0], (0, 2, 1))
    suffix = carried_in((flipped, local_term), "ctx", combine, (eye_stack, zero_stack))
    mixer_grads = pull_mixer((grad_mixed, suffix[1]))
    unused_five, pull_feat = jax.vjp(features, extended, tap_values, gate_logits, a_log, dt_bias)
    grad_ext, grad_taps, grad_logits, grad_alog, grad_bias = pull_feat(mixer_grads[1:])
    returned = from_behind(grad_ext[: CONV - 1], "ctx", -1)
    grad_conv = grad_ext[CONV - 1 :].at[count - (CONV - 1) :].add(returned)
    grad_proj = jnp.concatenate([grad_conv, grad_gate_out], axis=1).astype(jnp.bfloat16)
    grad_in = jnp.dot(grad_proj.T, normed_in, preferred_element_type=jnp.float32)
    grad_normed = jnp.dot(grad_proj, w_in, preferred_element_type=jnp.float32) + jnp.dot(
        grad_logits, w_gates.T, precision=HIGHEST
    )
    grad_gates = jnp.dot(normed_in.astype(jnp.float32).T, grad_logits, precision=HIGHEST)
    unused_six, pull_in = jax.vjp(norm_scale, x_float, gain_one)
    grad_x, grad_gain_one = pull_in(grad_normed)
    grad_input = (grad_resid + grad_x).astype(jnp.bfloat16)
    mix_flat = jnp.concatenate([grad_in, grad_out], axis=0).reshape(-1)
    mix_shard = lax.psum_scatter(mix_flat, ("dp", "ctx"), scatter_dimension=0, tiled=True)
    small_local = jnp.concatenate(
        [
            grad_gain_one,
            grad_gain_two,
            grad_gain_head,
            grad_taps.reshape(-1),
            grad_gates.reshape(-1),
            grad_alog,
            grad_bias,
        ]
    )
    shard_squares = jnp.sum(mix_shard * mix_shard) + jnp.sum(ffn_shard * ffn_shard)
    small_grad, total_squares = lax.psum((small_local, shard_squares), ("dp", "ctx"))
    squares = total_squares + jnp.sum(small_grad * small_grad)
    clip = jnp.minimum(1.0, MAX_NORM / (jnp.sqrt(squares) + 1e-06))
    mixer_new, mixer_first_new, mixer_second_new = adam_step(
        mixer_params, mix_shard, mixer_first, mixer_second, clip
    )
    ffn_new, ffn_first_new, ffn_second_new = adam_step(
        ffn_params, ffn_shard, ffn_first, ffn_second, clip
    )
    small_new, small_first_new, small_second_new = adam_step(
        small_params, small_grad, small_first, small_second, clip
    )
    return (
        result[None],
        grad_input[None],
        mix_shard,
        ffn_shard,
        small_grad,
        mixer_new,
        mixer_first_new,
        mixer_second_new,
        ffn_new,
        ffn_first_new,
        ffn_second_new,
        small_new,
        small_first_new,
        small_second_new,
    )


def solution(mesh):
    return jax.shard_map(
        body,
        mesh=mesh,
        in_specs=(
            P("dp", "ctx", None),
            P("dp", "ctx", None),
            P(("dp", "ctx")),
            P(("dp", "ctx")),
            P(("dp", "ctx")),
            P(("dp", "ctx")),
            P(("dp", "ctx")),
            P(("dp", "ctx")),
            P(),
            P(),
            P(),
        ),
        out_specs=(
            P("dp", "ctx", None),
            P("dp", "ctx", None),
            P(("dp", "ctx")),
            P(("dp", "ctx")),
            P(),
            P(("dp", "ctx")),
            P(("dp", "ctx")),
            P(("dp", "ctx")),
            P(("dp", "ctx")),
            P(("dp", "ctx")),
            P(("dp", "ctx")),
            P(),
            P(),
            P(),
        ),
        check_vma=False,
    )
```

profile of v0, /device:TPU:0, one launch (start us, length us, event | category | flops | bytes accessed | tf_op | source)
XLA Modules:
  0.0 1128.1 jit_solution(17236866343093623935)
XLA Ops:
  13.7 77.5 %all-gather.11.cloned.1.call-done = bf16[4194304]{0:T(1024)(128)(2,1)} async-done(((bf16[131072]{0:T(1024)(128)(2,1)}), bf16[4194304]{0:T(1024)(128)(2,1)}) %all-gather.11.cloned.1.call-update) | async-done | bytes 8388624 | tf_op jit(solution)/shard_map/all_gather | solution.py:269
  91.2 6.4 slice.294
  97.7 10.3 slice.251
  108.0 5.0 fusion.320
  113.0 2.2 collective-permute-start
  121.7 38.8 %while.160 = (s32[]{:T(128)}, f32[2,256,256]{2,1,0:T(8,128)}, f32[2,256,512]{2,1,0:T(8,128)}, f32[2,2,64]{2,1,0:T(2,128)}, f32[2,2,64,256]{3,2,1,0:T(8,128)S(1)}...) while((s32[]{:T(128)}, f32[2,256,256]{2,1,0:T(8,128)}, ...), condition=%wide.region_4.6_spmd.clone, body=%wide.region_2.5_spmd.clone.sunk | while | flops 1611903232 | bytes 17252060 | solution.py:229
  124.1 9.8 custom-call.53
  139.0 2.0 convolution_add_fusion.36
  143.5 9.8 custom-call.53
  158.4 2.0 convolution_add_fusion.36
  160.5 2.0 convert_element_type.132
  162.5 2.1 convert_element_type.133
  167.9 3.2 slice.305
  171.1 4.2 slice.267
  175.4 4.2 slice.275
  183.7 6.1 slice.306
  189.8 9.7 slice.270
  199.5 3.0 slice.309
  202.5 5.5 slice.274
  208.1 31.5 %all-gather.17.cloned.1.call-done = bf16[16,256,512]{2,1,0:T(8,128)(2,1)} async-done(((bf16[2,256,512]{2,1,0:T(8,128)(2,1)}), bf16[16,256,512]{2,1,0:T(8,128)(2,1)}) %all-gather.17.cloned.1.call-update) | async-done | bytes 4194320 | tf_op jit(solution)/shard_map/all_gather | solution.py:34
  239.6 16.6 %while.161 = (s32[]{:T(128)}, f32[2,256,512]{2,1,0:T(8,128)S(1)}, s32[]{:T(128)}, bf16[8,2,256,256]{3,2,1,0:T(8,128)(2,1)}, bf16[8,2,256,512]{3,2,1,0:T(8,128)(2,1)}, /*index=5*/s32[]{:T(128)}, s32[]{:T(128)}) while((s32[]{:T(128)}, f32[2,256,512]{2,1,0:T(8,128)S(1)}, s32[]{:T(128)}, bf16[8,2,256,256]{3,2,1,0:T(8,128)(2,1)}, ...), condition=%wide.region_6.8_spmd.clone, body=%wide.region_5.7_spmd.clone.sunk | while | flops 806617088 | bytes 6031975 | solution.py:51
  243.8 2.0 fusion.546
  248.0 2.0 fusion.546
  252.2 2.0 fusion.546
  254.2 2.0 fusion.546
  257.2 52.2 %while.156 = (s32[]{:T(128)}, f32[2,256,512]{2,1,0:T(8,128)S(1)}, f32[2,2,64,512]{3,2,1,0:T(8,128)}, f32[2,2,64]{2,1,0:T(2,128)}, f32[2,2,64,256]{3,2,1,0:T(8,12...) while((s32[]{:T(128)}, f32[2,256,512]{2,1,0:T(8,128)S(1)}, ...), condition=%wide.region_10.12_spmd, body=%wide.region_8.11_spmd.sunk | while | flops 781201600 | bytes 15008757 | solution.py:198
  260.1 2.4 fusion.477
  266.8 11.2 custom-call.50
  286.3 2.4 fusion.477
  292.9 11.2 custom-call.50
  311.3 2.0 multiply_convert_fusion.3
  315.2 3.0 multiply_reduce_fusion.9
  321.2 69.0 %while.158 = (s32[]{:T(128)}, f32[2,256,512]{2,1,0:T(8,128)S(1)}, f32[2,2,64,64]{3,2,1,0:T(8,128)}, f32[2,2,64,64]{3,2,1,0:T(8,128)}, f32[2,2,64,1]{2,1,3,0:T(2,...) while((s32[]{:T(128)}, f32[2,256,512]{2,1,0:T(8,128)S(1)}, ...), condition=%wide.region_17.19_spmd.clone.clone, body=%wide.region_15.18_spmd.clone.clone.sunk | while | flops 529560128 | bytes 10886193 | solution.py:198
  330.0 11.2 custom-call.51
  341.2 2.2 bitcast_dynamic-update-slice_fusion.18
  359.6 11.2 custom-call.51
  370.8 2.2 bitcast_dynamic-update-slice_fusion.18
  390.2 5.0 fusion.317
  402.4 15.0 %while.162 = (s32[]{:T(128)}, f32[2,256,512]{2,1,0:T(8,128)S(1)}, f32[2,2,1,1]{1,3,2,0:T(1,128)}, f32[2,2,64,256]{3,2,1,0:T(8,128)}, f32[2,2,64,512]{3,2,1,0:T(8...) while((s32[]{:T(128)}, f32[2,256,512]{2,1,0:T(8,128)S(1)}, ...), condition=%wide.region_19.21_spmd.clone, body=%wide.region_18.20_spmd.clone.sunk | while | flops 655753216 | bytes 7277727 | solution.py:198
  403.0 2.0 convolution_add_fusion.37
  410.6 2.0 convolution_add_fusion.37
  420.2 3.4 fusion.289
  425.4 5.7 maximum_bitcast_fusion
  431.1 8.3 copy.331
  439.4 2.7 fusion.296
  442.2 12.9 %all-gather.21.cloned.1.call-done = bf16[16,256,512]{2,1,0:T(8,128)(2,1)} async-done(((bf16[2,256,512]{2,1,0:T(8,128)(2,1)}), bf16[16,256,512]{2,1,0:T(8,128)(2,1)}) %all-gather.21.cloned.1.call-update) | async-done | bytes 4194320 | tf_op jit(solution)/shard_map/all_gather | solution.py:59
  455.3 13.4 %while.157 = (s32[]{:T(128)}, f32[2,256,512]{2,1,0:T(8,128)S(1)}, s32[]{:T(128)}, bf16[8,2,256,256]{3,2,1,0:T(8,128)(2,1)}, bf16[8,2,256,512]{3,2,1,0:T(8,128)(2...) while((s32[]{:T(128)}, f32[2,256,512]{2,1,0:T(8,128)S(1)}, s32[]{:T(128)}, ...), condition=%wide.region_21.23_spmd, body=%wide.region_20.22_spmd.sunk | while | flops 805830656 | bytes 4981907 | solution.py:76
  472.2 67.0 %while.159 = (s32[]{:T(128)}, f32[2,256,512]{2,1,0:T(8,128)S(1)}, f32[2,2,64,256]{3,2,0,1:T(8,128)}, f32[2,2,64,256]{3,2,0,1:T(8,128)}, f32[2,2,64,512]{3,2,0,1:...) while((s32[]{:T(128)}, f32[2,256,512]{2,1,0:T(8,128)S(1)}, ...), condition=%wide.region_33.35_spmd.clone.clone, body=%wide.region_22.34_spmd.clone.clone.sunk | while | flops 1569133696 | bytes 51536812 | solution.py:198
  479.0 9.8 custom-call.52
  489.3 2.1 fusion.517
  492.1 2.1 convolution_add_fusion.32
  494.3 2.0 convolution_add_fusion.34
  512.3 9.8 custom-call.52
  522.7 2.1 fusion.517
  525.5 2.1 convolution_add_fusion.32
  527.6 2.0 convolution_add_fusion.34
  551.6 5.3 maximum_bitcast_fusion.1
  556.9 8.1 copy.330
  566.2 3.1 fusion.238
  570.7 3.9 fusion.274
  576.6 491.6 %all-reduce.22.cloned.1.call-done = (f32[4194304]{0:T(1024)}, f32[4325376]{0:T(1024)}) async-done(((f32[4194304]{0:T(1024)}, f32[4325376]{0:T(1024)}), (f32[4194304]{0:T(1024)}, f32[4325376]{0:T(1024)})) %all-reduce.22.cloned.1.call-update) | async-done | bytes 34078736
  1069.9 2.0 multiply_reduce_fusion.4
  1073.2 40.8 %all-reduce.18 = (f32[14852]{0:T(1024)S(1)}, f32[]{:T(128)}) all-reduce(f32[14852]{0:T(1024)S(1)} %concatenate.40, f32[]{:T(128)S(6)} %add.447), channel_id=1, replica_groups=mesh['dp'=4,'ctx'=8] {'dp','ctx'}, use_global_device_ids=true, to_apply=%region_48.50 | all-reduce | flops 14853 | bytes 118824 | tf_op jit(solution)/shard_map/psum | solution.py:350
  1116.7 2.6 multiply_subtract_fusion.1
  (715 shorter events, 202.0 us)
Async XLA Ops:
  7.2 4.4 copy-start.11
  7.2 84.0 %all-gather.11.cloned.1.call-start = ((), (), s32[]{:S(2)}) async-start(), calls=%async_computation | async-start | bytes 8650752 | tf_op jit(solution)/shard_map/all_gather | solution.py:269
  9.1 174.6 %all-gather.13.cloned.1.call-start = ((), (), s32[]{:S(2)}) async-start(), calls=%async_computation.1 | async-start | bytes 8921088 | tf_op jit(solution)/shard_map/all_gather | solution.py:270
  10.9 197.1 %all-gather.15.cloned.1.call-start = ((), (), s32[]{:S(2)}) async-start(), calls=%async_computation.2 | async-start | bytes 2359296 | tf_op jit(solution)/shard_map/all_gather | solution.py:34
  11.6 86.1 %copy-start.28 = (f32[1024,4]{1,0:T(8,128)}, f32[1024,4]{1,0:T(8,128)S(1)}, u32[]{:S(2)}) copy-start(f32[1024,4]{1,0:T(8,128)S(1)} %reshape.844) | copy-start | bytes 49156
  11.7 96.3 %copy-start.95 = (f32[128]{0:T(128)}, f32[128]{0:T(128)S(1)}, u32[]{:S(2)}) copy-start(f32[128]{0:T(128)S(1)} %fusion.309) | copy-start | bytes 1540
  11.8 85.9 %copy-start.121 = (f32[2]{0:T(128)}, f32[2]{0:T(128)S(1)}, u32[]{:S(2)}) copy-start(f32[2]{0:T(128)S(1)} %get-tuple-element.2850) | copy-start | bytes 28
  11.8 85.9 %copy-start.123 = (f32[2]{0:T(128)}, f32[2]{0:T(128)S(1)}, u32[]{:S(2)}) copy-start(f32[2]{0:T(128)S(1)} %get-tuple-element.2851) | copy-start | bytes 28
  12.4 95.6 %copy-start.69 = (f32[1024]{0:T(1024)}, f32[1024]{0:T(1024)S(1)}, u32[]{:S(2)}) copy-start(f32[1024]{0:T(1024)S(1)} %get-tuple-element.2845) | copy-start | bytes 12292
  13.0 84.7 %copy-start.98 = (f32[128,4]{0,1:T(4,128)}, f32[128,4]{0,1:T(4,128)S(1)}, u32[]{:S(2)}) copy-start(f32[128,4]{0,1:T(4,128)S(1)} %fusion.282) | copy-start | bytes 6148
  13.6 102.3 %copy-start.113 = (f32[128,2]{0,1:T(2,128)}, f32[128,2]{0,1:T(2,128)S(1)}, u32[]{:S(2)}) copy-start(f32[128,2]{0,1:T(2,128)S(1)} %get-tuple-element.2853) | copy-start | bytes 3076
  13.7 103.1 %copy-start.77 = (f32[2048]{0:T(1024)}, f32[2048]{0:T(1024)S(1)}, u32[]{:S(2)}) copy-start(f32[2048]{0:T(1024)S(1)} %get-tuple-element.2846) | copy-start | bytes 24580
  13.7 103.1 %copy-start.79 = (f32[2048]{0:T(1024)}, f32[2048]{0:T(1024)S(1)}, u32[]{:S(2)}) copy-start(f32[2048]{0:T(1024)S(1)} %get-tuple-element.2847) | copy-start | bytes 24580
  13.7 103.1 %copy-start.81 = (f32[2048]{0:T(1024)}, f32[2048]{0:T(1024)S(1)}, u32[]{:S(2)}) copy-start(f32[2048]{0:T(1024)S(1)} %get-tuple-element.2848) | copy-start | bytes 24580
  13.7 103.1 %copy-start.83 = (f32[2048]{0:T(1024)}, f32[2048]{0:T(1024)S(1)}, u32[]{:S(2)}) copy-start(f32[2048]{0:T(1024)S(1)} %get-tuple-element.2849) | copy-start | bytes 24580
  113.0 5.4 copy-start.15
  113.0 3.7 collective-permute-start
  162.5 77.1 %all-gather.17.cloned.1.call-start = ((), (), s32[]{:S(2)}) async-start(), calls=%async_computation.3 | async-start | bytes 4718592 | tf_op jit(solution)/shard_map/all_gather | solution.py:34
  164.6 277.5 %all-gather.19.cloned.1.call-start = ((), (), s32[]{:S(2)}) async-start(), calls=%async_computation.4 | async-start | bytes 2359296 | tf_op jit(solution)/shard_map/all_gather | solution.py:59
  183.3 271.7 %all-gather.21.cloned.1.call-start = ((), (), s32[]{:S(2)}) async-start(), calls=%async_computation.5 | async-start | bytes 4718592 | tf_op jit(solution)/shard_map/all_gather | solution.py:59
  258.1 7.0 copy-start.62
  284.2 7.0 copy-start.62
  309.4 5.8 copy-start.12
  313.3 7.9 copy-start.3
  313.3 7.9 copy-start.5
  343.4 5.1 copy-start.73
  344.9 4.4 copy-start.23
  344.9 5.1 copy-start.93
  344.9 5.1 copy-start.131
  373.1 5.1 copy-start.73
  374.5 4.4 copy-start.23
  374.5 5.1 copy-start.93
  374.5 5.1 copy-start.131
  390.1 5.0 copy-start.14
  390.1 5.0 copy-start.55
  390.2 6.9 slice-start
  418.3 649.8 %all-reduce.22.cloned.1.call-start = ((), (), s32[]{:S(2)}) async-start(), calls=%async_computation.6 | async-start | bytes 68157440
  431.1 8.4 copy-start.26
  431.1 8.3 copy-start.39
  455.2 16.9 %copy-start.42 = (pred[64,64]{1,0:T(8,128)(4,1)S(1)}, pred[64,64]{1,0:T(8,128)(4,1)}, u32[]{:S(2)}) copy-start(pred[64,64]{1,0:T(8,128)(4,1)} %get-tuple-element.3960) | copy-start | bytes 12292
  455.2 16.9 %copy-start.87 = (f32[2,2,64]{2,1,0:T(2,128)S(1)}, f32[2,2,64]{2,1,0:T(2,128)}, u32[]{:S(2)}) copy-start(f32[2,2,64]{2,1,0:T(2,128)} %get-tuple-element.3846) | copy-start | bytes 3076
  455.2 16.9 %copy-start.90 = (f32[2,2,64]{2,1,0:T(2,128)S(1)}, f32[2,2,64]{2,1,0:T(2,128)}, u32[]{:S(2)}) copy-start(f32[2,2,64]{2,1,0:T(2,128)} %get-tuple-element.3848) | copy-start | bytes 3076
  455.2 16.9 %copy-start.104 = (f32[2,2,64,1]{2,1,3,0:T(2,128)S(1)}, f32[2,2,64,1]{2,1,3,0:T(2,128)}, u32[]{:S(2)}) copy-start(f32[2,2,64,1]{2,1,3,0:T(2,128)} %get-tuple-element.3843) | copy-start | bytes 3076
  455.2 16.9 %copy-start.107 = (f32[2,2,64,1]{2,1,3,0:T(2,128)S(1)}, f32[2,2,64,1]{2,1,3,0:T(2,128)}, u32[]{:S(2)}) copy-start(f32[2,2,64,1]{2,1,3,0:T(2,128)} %get-tuple-element.3842) | copy-start | bytes 3076
  472.4 4.5 copy-start
  494.3 4.4 copy-start.35
  505.8 4.5 copy-start
  527.6 4.4 copy-start.35
  539.1 5.3 copy-start.47
  546.1 3.1 collective-permute-start.1
  565.1 4.4 copy-start.119
  566.2 4.4 copy-start.66
  570.7 4.8 copy-start.97
  570.7 4.8 copy-start.126
  570.7 4.9 copy-start.128
  575.5 540.5 %copy-start.91 = (f32[14852]{0:T(1024)S(1)}, f32[14852]{0:T(1024)}, u32[]{:S(2)}) copy-start(f32[14852]{0:T(1024)} %param.38) | copy-start | bytes 178228
  575.5 540.5 %copy-start.92 = (f32[14852]{0:T(1024)S(1)}, f32[14852]{0:T(1024)}, u32[]{:S(2)}) copy-start(f32[14852]{0:T(1024)} %param.39) | copy-start | bytes 178228
  575.7 541.0 %copy-start.50 = (f32[131072]{0:T(1024)S(1)}, f32[131072]{0:T(1024)}, u32[]{:S(2)}) copy-start(f32[131072]{0:T(1024)} %param.31) | copy-start | bytes 1572868
  1069.9 49.4 %copy-start.44 = (f32[131072]{0:T(1024)}, f32[131072]{0:T(1024)S(1)}, u32[]{:S(2)}) copy-start(f32[131072]{0:T(1024)S(1)} %get-tuple-element.2774) | copy-start | bytes 1572868
  1071.9 47.4 %copy-start.41 = (f32[135168]{0:T(1024)}, f32[135168]{0:T(1024)S(1)}, u32[]{:S(2)}) copy-start(f32[135168]{0:T(1024)S(1)} %get-tuple-element.2772) | copy-start | bytes 1622020
  1114.0 6.8 copy-start.64
  1114.0 5.3 copy-start.40
  1114.0 5.3 copy-start.60
  1114.0 5.3 copy-start.61
  (119 other events, 295.1 us)
Sparse Core Ops, SparseCore 0:
  11.4 79.7 all-gather.10
  94.7 76.8 all-gather.12
  174.1 26.4 all-gather.14
  203.0 36.5 all-gather.16
  241.3 27.8 all-gather.18
  418.4 36.6 all-gather.20
  565.2 502.9 all-reduce.21
where the time goes:
time: 1140 us; the launch traced here: 1130 us
  waiting for transfers between devices  615 us (54%)
  other arithmetic  166 us (15%)
  matrix products  152 us (13%)
  local copies, waits for them, and re-layouts  120 us (11%)
  blocking collectives  40.8 us (4%)
  between operations  18.7 us (2%)
  loops' own time  12 us (1%)
    unnamed x8, waiting for transfers between devices  492 us
    another operation x34, other arithmetic, group_parts(): jax.scipy.linalg.solve_triangular(system, right_side, lower=True, unit_di...  86.5 us
    all_gather x1, waiting for transfers between devices, body(): lax.all_gather(mix_part, ('dp', 'ctx'), axis=0, tiled=True)  77.5 us
    psum x1, blocking collectives, body(): lax.psum((small_local, shard_squares), ('dp', 'ctx'))  40.8 us
    dot_general x17, matrix products, combine(): jnp.einsum('hij,hjk->hik', second_map, first_shift, precision=HIGHEST)  32.5 us
    all_gather x2, waiting for transfers between devices, entering(): lax.all_gather(part.astype(kind), axis)  31.5 us
  transfers between devices with their start and end apart: 9, of which 5 were waited for; matrix products, arithmetic and copies ran while one was open for 28% of the time, Pallas kernels for 0%

commit v1 on v0

--- a/solution.py
+++ b/solution.py
@@ -1,3 +1,4 @@
+import functools
 import jax
 import jax.numpy as jnp
 from jax import lax
@@ -20,6 +21,28 @@
 CORRECT_TWO = 1.0 - 0.999**3
 MAX_NORM = 1.0
 HIGHEST = lax.Precision.HIGHEST
+
+
+def map_recover(field_in, axis_name):
+    spare, v_now, z = (jax.lax.psum(1, axis_name), jax.lax.axis_index(axis_name), field_in.shape[0])
+    all_rows, raw_out = (field_in, 1)
+    while raw_out < spare:
+        all_rows = jnp.concatenate(
+            [
+                all_rows,
+                jax.lax.ppermute(
+                    all_rows,
+                    axis_name,
+                    list(map(lambda d: (d, (d - raw_out) % spare), range(spare))),
+                ),
+            ],
+            0,
+        )
+        raw_out = 2 * raw_out
+    return jnp.roll(all_rows, v_now * z, 0)
+
+
+_use_blocks = functools.partial(map_recover, axis_name=("dp", "ctx"))
 
 
 def from_behind(value, axis, steps):
@@ -266,7 +289,7 @@
     mix_part = mixer_params.astype(jnp.bfloat16)
     ffn_part = ffn_params.astype(jnp.bfloat16)
     mix_whole, ffn_whole = (
-        lax.all_gather(mix_part, ("dp", "ctx"), axis=0, tiled=True),
+        _use_blocks(mix_part),
         lax.all_gather(ffn_part, ("dp", "ctx"), axis=0, tiled=True),
     )
     w_in, w_out, w_ffn, w_down = split_weights(mix_whole, ffn_whole)

time: 1140 us -> 1380 us (1.21)
  waiting for transfers between devices: 615 us -> 804 us
  local copies, waits for them, and re-layouts: 120 us -> 159 us
    ppermute x0 -> x5, waiting for transfers between devices: none -> 258 us  [map_recover(): jax.lax.ppermute(all_rows, axis_name, list(map(lambda d: (d, (d - raw_out...]
    all_gather x1 -> x0, waiting for transfers between devices: 77.5 us -> none  [body(): lax.all_gather(mix_part, ('dp', 'ctx'), axis=0, tiled=True)]
    unnamed x198 -> x196, local copies, waits for them, and re-layouts: 21.3 us -> 36.5 us
    all_gather x2, waiting for transfers between devices: 31.5 us -> 46.1 us  [entering(): lax.all_gather(part.astype(kind), axis)]
    unnamed x8 -> x7, waiting for transfers between devices: 492 us -> 487 us
  transfers between devices with their start and end apart: 9 -> 13, of which waited for: 5 -> 10; matrix products, arithmetic and copies ran while one was open for 28% -> 20% of each run, Pallas kernels for 0% -> 0%
where the time goes in v1:
time: 1380 us; the launch traced here: 1370 us
  waiting for transfers between devices  804 us (58%)
  other arithmetic  172 us (12%)
  local copies, waits for them, and re-layouts  159 us (12%)
  matrix products  156 us (11%)
  blocking collectives  40.8 us (3%)
  between operations  18.5 us (1%)
  starting transfers between devices  15.3 us (1%)
    unnamed x7, waiting for transfers between devices  487 us
    ppermute x5, waiting for transfers between devices, map_recover(): jax.lax.ppermute(all_rows, axis_name, list(map(lambda d: (d, (d - raw_out...  258 us
    another operation x34, other arithmetic, group_parts(): jax.scipy.linalg.solve_triangular(system, right_side, lower=True, unit_di...  86.5 us
    all_gather x2, waiting for transfers between devices, entering(): lax.all_gather(part.astype(kind), axis)  46.1 us
    psum x1, blocking collectives, body(): lax.psum((small_local, shard_squares), ('dp', 'ctx'))  40.8 us
    unnamed x196, local copies, waits for them, and re-layouts  36.5 us
    dot_general x17, matrix products, combine(): jnp.einsum('hij,hjk->hik', second_map, first_shift, precision=HIGHEST)  32.6 us
  transfers between devices with their start and end apart: 13, of which 10 were waited for; matrix products, arithmetic and copies ran while one was open for 20% of the time, Pallas kernels for 0%

profile of v1, /device:TPU:0, one launch (start us, length us, event | category | flops | bytes accessed | tf_op | source)
XLA Modules:
  0.0 1366.6 jit_solution(3357960069091709359)
XLA Ops:
  9.0 6.4 collective-permute-start
  16.2 3.1 collective-permute-done
  20.8 9.9 collective-permute-done.1
  32.6 23.5 %collective-permute-done.2 = bf16[524288]{0:T(1024)(128)(2,1)S(1)} collective-permute-done((bf16[524288]{0:T(1024)(128)(2,1)S(1)}, bf16[524288]{0:T(1024)(128)(2,1)S(1)}, u32[]{:S(2)}, u32[]{:S(2)}) %collective-permute-start.2) | collective-permute-done | bytes 1048608 | tf_op jit(solution)/shard_map/ppermute | solution.py:33
  56.3 3.2 collective-permute-start.3
  60.9 43.5 %collective-permute-done.3 = bf16[1048576]{0:T(1024)(128)(2,1)S(1)} collective-permute-done((bf16[1048576]{0:T(1024)(128)(2,1)S(1)}, bf16[1048576]{0:T(1024)(128)(2,1)S(1)}, u32[]{:S(2)}, u32[]{:S(2)}) %collective-permute-start.3) | collective-permute-done | bytes 2097184 | tf_op jit(solution)/shard_map/ppermute | solution.py:33
  105.7 2.4 constant_dynamic-update-slice_fusion.10
  113.0 177.4 %collective-permute-done.4 = bf16[2097152]{0:T(1024)(128)(2,1)} collective-permute-done((bf16[2097152]{0:T(1024)(128)(2,1)}, bf16[2097152]{0:T(1024)(128)(2,1)}, u32[]{:S(2)}, u32[]{:S(2)}) %collective-permute-start.4) | collective-permute-done | bytes 4194336 | tf_op jit(solution)/shard_map/ppermute | solution.py:33
  290.4 3.8 constant_dynamic-update-slice_fusion.26
  299.1 3.7 constant_dynamic-update-slice_fusion.20
  302.8 6.4 dynamic-slice.10
  309.3 10.3 slice.251
  319.6 5.0 fusion.320
  333.6 38.6 %while.160 = (s32[]{:T(128)}, f32[2,256,256]{2,1,0:T(8,128)}, f32[2,256,512]{2,1,0:T(8,128)}, f32[2,2,64]{2,1,0:T(2,128)}, f32[2,2,64,256]{3,2,1,0:T(8,128)S(1)}...) while((s32[]{:T(128)}, f32[2,256,256]{2,1,0:T(8,128)}, ...), condition=%wide.region_4.6_spmd.clone, body=%wide.region_2.5_spmd.clone.sunk | while | flops 1611903232 | bytes 17252060 | solution.py:252
  336.1 9.8 custom-call.57
  350.9 2.1 convolution_add_fusion.36
  355.4 9.8 custom-call.57
  370.2 2.1 convolution_add_fusion.36
  374.3 2.1 convert_element_type.133
  381.8 3.1 dynamic-slice.11
  384.9 4.2 slice.267
  389.1 4.2 slice.275
  397.2 7.0 all-gather.12.cloned.1.call-done
  404.2 39.1 %all-gather.14.cloned.1.call-done = bf16[16,256,512]{2,1,0:T(8,128)(2,1)} async-done(((bf16[2,256,512]{2,1,0:T(8,128)(2,1)}), bf16[16,256,512]{2,1,0:T(8,128)(2,1)}) %all-gather.14.cloned.1.call-update) | async-done | bytes 4194320 | tf_op jit(solution)/shard_map/all_gather | solution.py:57
  443.3 16.6 %while.161 = (s32[]{:T(128)}, f32[2,256,512]{2,1,0:T(8,128)S(1)}, s32[]{:T(128)}, bf16[8,2,256,256]{3,2,1,0:T(8,128)(2,1)}, bf16[8,2,256,512]{3,2,1,0:T(8,128)(2,1)}, /*index=5*/s32[]{:T(128)}, s32[]{:T(128)}) while((s32[]{:T(128)}, f32[2,256,512]{2,1,0:T(8,128)S(1)}, s32[]{:T(128)}, bf16[8,2,256,256]{3,2,1,0:T(8,128)(2,1)}, ...), condition=%wide.region_6.8_spmd.clone, body=%wide.region_5.7_spmd.clone.sunk | while | flops 806617088 | bytes 6031975 | solution.py:74
  460.9 54.5 %while.156 = (s32[]{:T(128)}, f32[2,256,512]{2,1,0:T(8,128)S(1)}, f32[2,2,64,512]{3,2,1,0:T(8,128)}, f32[2,2,64]{2,1,0:T(2,128)}, f32[2,2,64,256]{3,2,1,0:T(8,12...) while((s32[]{:T(128)}, f32[2,256,512]{2,1,0:T(8,128)S(1)}, ...), condition=%wide.region_10.12_spmd, body=%wide.region_8.11_spmd.sunk | while | flops 781201600 | bytes 15006109 | solution.py:221
  463.8 2.4 fusion.477
  470.4 11.2 custom-call.54
  484.7 2.0 convolution_add_fusion.29
  491.0 2.4 fusion.477
  497.7 11.2 custom-call.54
  511.9 2.0 convolution_add_fusion.29
  520.5 3.0 multiply_reduce_fusion.9
  526.6 65.1 %while.158 = (s32[]{:T(128)}, f32[2,256,512]{2,1,0:T(8,128)S(1)}, f32[2,2,64,64]{3,2,1,0:T(8,128)}, f32[2,2,64,64]{3,2,1,0:T(8,128)}, f32[2,2,64,1]{2,1,3,0:T(2,...) while((s32[]{:T(128)}, f32[2,256,512]{2,1,0:T(8,128)S(1)}, ...), condition=%wide.region_17.19_spmd.clone.clone, body=%wide.region_15.18_spmd.clone.clone.sunk | while | flops 529560128 | bytes 10851429 | solution.py:221
  535.5 11.2 custom-call.55
  546.7 2.2 bitcast_dynamic-update-slice_fusion.18
  568.1 11.2 custom-call.55
  579.3 2.2 bitcast_dynamic-update-slice_fusion.18
  591.7 6.1 slice.304
  597.8 9.7 slice.270
  607.5 3.1 slice.307
  610.6 15.2 %slice.274 = bf16[1408,1024]{1,0:T(8,128)(2,1)} reshape(bf16[1441792]{0:T(1024)(128)(2,1)} %slice.307) | data formatting | bytes 5767168 | tf_op jit(solution)/shard_map/slice | solution.py:133
  625.8 4.8 fusion.317
  635.0 2.4 multiply_reduce_fusion.6
  637.7 15.0 %while.162 = (s32[]{:T(128)}, f32[2,256,512]{2,1,0:T(8,128)S(1)}, f32[2,2,1,1]{1,3,2,0:T(1,128)}, f32[2,2,64,256]{3,2,1,0:T(8,128)}, f32[2,2,64,512]{3,2,1,0:T(8...) while((s32[]{:T(128)}, f32[2,256,512]{2,1,0:T(8,128)S(1)}, ...), condition=%wide.region_19.21_spmd.clone, body=%wide.region_18.20_spmd.clone.sunk | while | flops 655753216 | bytes 7277727 | solution.py:221
  655.4 4.5 fusion.288
  661.6 5.8 maximum_bitcast_fusion
  667.4 8.3 copy.331
  675.8 2.7 fusion.295
  678.5 12.1 all-gather.18.cloned.1.call-done
  690.7 13.4 while.157
  707.6 67.0 %while.159 = (s32[]{:T(128)}, f32[2,256,512]{2,1,0:T(8,128)S(1)}, f32[2,2,64,256]{3,2,0,1:T(8,128)}, f32[2,2,64,256]{3,2,0,1:T(8,128)}, f32[2,2,64,512]{3,2,0,1:...) while((s32[]{:T(128)}, f32[2,256,512]{2,1,0:T(8,128)S(1)}, ...), condition=%wide.region_33.35_spmd.clone.clone, body=%wide.region_22.34_spmd.clone.clone.sunk | while | flops 1569133696 | bytes 51536812 | solution.py:221
  714.4 9.8 custom-call.56
  724.7 2.3 fusion.517
  727.8 2.0 convolution_add_fusion.32
  747.7 9.8 custom-call.56
  758.1 2.3 fusion.517
  789.2 5.3 maximum_bitcast_fusion.1
  794.6 8.1 copy.330
  803.8 3.1 fusion.238
  811.2 4.7 fusion.256
  819.1 486.7 %all-reduce.22.cloned.1.call-done = (f32[4194304]{0:T(1024)}, f32[4325376]{0:T(1024)}) async-done(((f32[4194304]{0:T(1024)}, f32[4325376]{0:T(1024)}), (f32[4194304]{0:T(1024)}, f32[4325376]{0:T(1024)})) %all-reduce.22.cloned.1.call-update) | async-done | bytes 34078736
  1310.9 40.8 %all-reduce.18 = (f32[14852]{0:T(1024)S(1)}, f32[]{:T(128)}) all-reduce(f32[14852]{0:T(1024)S(1)} %concatenate.67, f32[]{:T(128)S(6)} %add.463), channel_id=1, replica_groups=mesh['dp'=4,'ctx'=8] {'dp','ctx'}, use_global_device_ids=true, to_apply=%region_48.50 | all-reduce | flops 14853 | bytes 118824 | tf_op jit(solution)/shard_map/psum | solution.py:373
  1355.2 2.6 multiply_subtract_fusion.1
  (673 shorter events, 250.6 us)
Async XLA Ops:
  7.2 397.0 %all-gather.12.cloned.1.call-start = ((), (), s32[]{:S(2)}) async-start(), calls=%async_computation.1 | async-start | bytes 2359296 | tf_op jit(solution)/shard_map/all_gather | solution.py:57
  9.0 10.3 collective-permute-start
  19.3 11.3 collective-permute-start.1
  30.8 25.4 %collective-permute-start.2 = (bf16[524288]{0:T(1024)(128)(2,1)S(1)}, bf16[524288]{0:T(1024)(128)(2,1)S(1)}, u32[]{:S(2)}, u32[]{:S(2)}) collective-permute-start(bf16[524288]{0:T(1024)(128)(2,1)S(1)} %pad_maximum_fusion.2), channel_id=1, source_target_pairs={{0,28},{1,29},{2,30},{3,31},{4,0},{5,1},{6,2},{7,3},{8,4},{9,5},{1... | collective-permute-start | bytes 3145736 | tf_op jit(solution)/shard_map/ppermute | solution.py:33
  56.3 48.1 %collective-permute-start.3 = (bf16[1048576]{0:T(1024)(128)(2,1)S(1)}, bf16[1048576]{0:T(1024)(128)(2,1)S(1)}, u32[]{:S(2)}, u32[]{:S(2)}) collective-permute-start(bf16[1048576]{0:T(1024)(128)(2,1)S(1)} %pad_maximum_fusion), channel_id=1, source_target_pairs={{0,24},{1,25},{2,26},{3,27},{4,28},{5,29},{6,30},{7,31},{8,0},{9,1... | collective-permute-start | bytes 6291464 | tf_op jit(solution)/shard_map/ppermute | solution.py:33
  59.4 49.2 %copy-start.65 = (f32[14852]{0:T(1024)S(1)}, f32[14852]{0:T(1024)}, u32[]{:S(2)}) copy-start(f32[14852]{0:T(1024)} %param.37) | copy-start | bytes 178228
  60.9 48.3 %copy-start.11 = (bf16[1,128,1024]{2,1,0:T(8,128)(2,1)S(1)}, bf16[1,128,1024]{2,1,0:T(8,128)(2,1)}, u32[]{:S(2)}) copy-start(bf16[1,128,1024]{2,1,0:T(8,128)(2,1)} %param.29) | copy-start | bytes 786436
  108.2 182.3 %collective-permute-start.4 = (bf16[2097152]{0:T(1024)(128)(2,1)}, bf16[2097152]{0:T(1024)(128)(2,1)}, u32[]{:S(2)}, u32[]{:S(2)}) collective-permute-start(bf16[2097152]{0:T(1024)(128)(2,1)} %get-tuple-element.2837), channel_id=1, source_target_pairs={{0,16},{1,17},{2,18},{3,19},{4,20},{5,21},{6,22},{7,23},{8,24},{9,... | collective-permute-start | bytes 12582920 | tf_op jit(solution)/shard_map/ppermute | solution.py:33
  109.2 185.0 %copy-start.29 = (f32[1024,4]{1,0:T(8,128)}, f32[1024,4]{1,0:T(8,128)S(1)}, u32[]{:S(2)}) copy-start(f32[1024,4]{1,0:T(8,128)S(1)} %reshape.844) | copy-start | bytes 49156
  109.9 209.7 %copy-start.86 = (f32[128]{0:T(128)}, f32[128]{0:T(128)S(1)}, u32[]{:S(2)}) copy-start(f32[128]{0:T(128)S(1)} %fusion.309) | copy-start | bytes 1540
  110.6 209.0 %copy-start.68 = (f32[1024]{0:T(1024)}, f32[1024]{0:T(1024)S(1)}, u32[]{:S(2)}) copy-start(f32[1024]{0:T(1024)S(1)} %get-tuple-element.2854) | copy-start | bytes 12292
  113.0 214.4 %copy-start.75 = (f32[2048]{0:T(1024)}, f32[2048]{0:T(1024)S(1)}, u32[]{:S(2)}) copy-start(f32[2048]{0:T(1024)S(1)} %get-tuple-element.2855) | copy-start | bytes 24580
  113.0 214.4 %copy-start.77 = (f32[2048]{0:T(1024)}, f32[2048]{0:T(1024)S(1)}, u32[]{:S(2)}) copy-start(f32[2048]{0:T(1024)S(1)} %get-tuple-element.2856) | copy-start | bytes 24580
  113.0 214.4 %copy-start.79 = (f32[2048]{0:T(1024)}, f32[2048]{0:T(1024)S(1)}, u32[]{:S(2)}) copy-start(f32[2048]{0:T(1024)S(1)} %get-tuple-element.2857) | copy-start | bytes 24580
  113.0 214.4 %copy-start.81 = (f32[2048]{0:T(1024)}, f32[2048]{0:T(1024)S(1)}, u32[]{:S(2)}) copy-start(f32[2048]{0:T(1024)S(1)} %get-tuple-element.2858) | copy-start | bytes 24580
  324.6 2.8 collective-permute-start.5
  374.2 69.1 %all-gather.14.cloned.1.call-start = ((), (), s32[]{:S(2)}) async-start(), calls=%async_computation.2 | async-start | bytes 4718592 | tf_op jit(solution)/shard_map/all_gather | solution.py:57
  376.4 215.3 %all-gather.10.cloned.1.call-start = ((), (), s32[]{:S(2)}) async-start(), calls=%async_computation | async-start | bytes 8921088 | tf_op jit(solution)/shard_map/all_gather | solution.py:293
  378.5 300.0 %all-gather.16.cloned.1.call-start = ((), (), s32[]{:S(2)}) async-start(), calls=%async_computation.3 | async-start | bytes 2359296 | tf_op jit(solution)/shard_map/all_gather | solution.py:82
  384.9 8.4 copy-start.23
  397.1 293.4 %all-gather.18.cloned.1.call-start = ((), (), s32[]{:S(2)}) async-start(), calls=%async_computation.4 | async-start | bytes 4718592 | tf_op jit(solution)/shard_map/all_gather | solution.py:82
  515.4 11.1 copy-start.3
  515.4 11.2 copy-start.5
  546.7 8.6 copy-start.72
  579.3 8.5 copy-start.72
  610.6 15.2 %copy-start.9 = (f32[128,1024]{1,0:T(8,128)S(1)}, f32[128,1024]{1,0:T(8,128)}, u32[]{:S(2)}) copy-start(f32[128,1024]{1,0:T(8,128)} %get-tuple-element.2866) | copy-start | bytes 1572868
  610.6 15.2 %copy-start.73 = (f32[1024]{0:T(1024)S(1)}, f32[1024]{0:T(1024)}, u32[]{:S(2)}) copy-start(f32[1024]{0:T(1024)} %get-tuple-element.2853) | copy-start | bytes 12292
  610.6 15.2 %copy-start.102 = (f32[128]{0:T(128)S(1)}, f32[128]{0:T(128)}, u32[]{:S(2)}) copy-start(f32[128]{0:T(128)} %fusion.310) | copy-start | bytes 1540
  653.5 652.3 %all-reduce.22.cloned.1.call-start = ((), (), s32[]{:S(2)}) async-start(), calls=%async_computation.5 | async-start | bytes 68157440
  667.4 8.4 copy-start.27
  667.4 8.4 copy-start.40
  690.7 16.9 %copy-start.43 = (pred[64,64]{1,0:T(8,128)(4,1)S(1)}, pred[64,64]{1,0:T(8,128)(4,1)}, u32[]{:S(2)}) copy-start(pred[64,64]{1,0:T(8,128)(4,1)} %get-tuple-element.3973) | copy-start | bytes 12292
  690.7 16.9 %copy-start.83 = (f32[2,2,64]{2,1,0:T(2,128)S(1)}, f32[2,2,64]{2,1,0:T(2,128)}, u32[]{:S(2)}) copy-start(f32[2,2,64]{2,1,0:T(2,128)} %get-tuple-element.3856) | copy-start | bytes 3076
  690.7 16.9 %copy-start.84 = (f32[2,2,64]{2,1,0:T(2,128)S(1)}, f32[2,2,64]{2,1,0:T(2,128)}, u32[]{:S(2)}) copy-start(f32[2,2,64]{2,1,0:T(2,128)} %get-tuple-element.3858) | copy-start | bytes 3076
  690.7 16.9 %copy-start.91 = (f32[2,2,64,1]{2,1,3,0:T(2,128)S(1)}, f32[2,2,64,1]{2,1,3,0:T(2,128)}, u32[]{:S(2)}) copy-start(f32[2,2,64,1]{2,1,3,0:T(2,128)} %get-tuple-element.3853) | copy-start | bytes 3076
  690.7 16.8 %copy-start.92 = (f32[2,2,64,1]{2,1,3,0:T(2,128)S(1)}, f32[2,2,64,1]{2,1,3,0:T(2,128)}, u32[]{:S(2)}) copy-start(f32[2,2,64,1]{2,1,3,0:T(2,128)} %get-tuple-element.3852) | copy-start | bytes 3076
  724.2 7.6 copy-start.1
  724.7 9.0 copy-start.8
  724.7 9.4 copy-start.35
  727.1 7.7 copy-start.25
  727.7 7.5 copy-start.56
  727.7 7.5 copy-start.57
  727.7 7.5 copy-start.58
  727.8 7.5 copy-start.59
  757.6 7.7 copy-start.1
  758.1 9.0 copy-start.8
  758.1 9.4 copy-start.35
  760.4 7.7 copy-start.25
  761.2 7.5 copy-start.56
  761.2 7.5 copy-start.57
  761.2 7.5 copy-start.58
  761.2 7.5 copy-start.59
  774.6 7.4 copy-start.17
  774.6 7.4 copy-start.32
  774.6 7.4 copy-start.71
  783.5 3.2 collective-permute-start.6
  802.7 7.8 copy-start.30
  815.9 539.3 %copy-start.50 = (f32[131072]{0:T(1024)S(1)}, f32[131072]{0:T(1024)}, u32[]{:S(2)}) copy-start(f32[131072]{0:T(1024)} %param.31) | copy-start | bytes 1572868
  815.9 541.9 %copy-start.41 = (f32[135168]{0:T(1024)S(1)}, f32[135168]{0:T(1024)}, u32[]{:S(2)}) copy-start(f32[135168]{0:T(1024)} %param.34) | copy-start | bytes 1622020
  815.9 541.9 %copy-start.60 = (f32[135168]{0:T(1024)S(1)}, f32[135168]{0:T(1024)}, u32[]{:S(2)}) copy-start(f32[135168]{0:T(1024)} %param.35) | copy-start | bytes 1622020
  815.9 541.9 %copy-start.61 = (f32[135168]{0:T(1024)S(1)}, f32[135168]{0:T(1024)}, u32[]{:S(2)}) copy-start(f32[135168]{0:T(1024)} %param.36) | copy-start | bytes 1622020
  1307.6 51.7 %copy-start.45 = (f32[131072]{0:T(1024)}, f32[131072]{0:T(1024)S(1)}, u32[]{:S(2)}) copy-start(f32[131072]{0:T(1024)S(1)} %get-tuple-element.2774) | copy-start | bytes 1572868
  1309.6 49.7 %copy-start.42 = (f32[135168]{0:T(1024)}, f32[135168]{0:T(1024)S(1)}, u32[]{:S(2)}) copy-start(f32[135168]{0:T(1024)S(1)} %get-tuple-element.2772) | copy-start | bytes 1622020
  1351.7 7.6 copy-start.64
  (91 other events, 320.8 us)
Sparse Core Ops, SparseCore 0:
  374.3 29.8 all-gather.11
  406.7 36.5 all-gather.13
  446.8 78.5 all-gather.9
  527.1 26.7 all-gather.15
  653.6 36.8 all-gather.17
  802.8 502.9 all-reduce.21
